TPU v7x, 256 devices: a whole 4x4x8 slice. The times are simulated.
256 devices in a mesh: pipe: 4 (over x), expert: 16 (over z, core), dp: 4 (over y).
Axes of the slice: x: 4, y: 4, z: 8, core: 2. Of those that a mesh axis runs over, the one named last changes fastest.
Arguments:
- tokens: bfloat16 [4, 8192, 2048], P('pipe', ('expert', 'dp')), may hold values from -6 to 6
- cotangent: bfloat16 [4, 8192, 2048], P('pipe', ('expert', 'dp')), may hold values from -6 to 6
- norm_gain: float32 [4, 2048], P('pipe'), may hold values from 0.5 to 1.5
- first_ids: int32 [4, 8192, 2], P('pipe', ('expert', 'dp')), may hold values from 0 to 7, all different within a row; in each aligned block of 128 rows (0 to 127, 128 to 255, ..., all dimensions but the last counted through in order) at most 36 rows name the same one
- first_gates: float32 [4, 8192, 2], P('pipe', ('expert', 'dp')), may hold values from 0.1 to 1
- second_ids: int32 [4, 8192, 2], P('pipe', ('expert', 'dp')), may hold values from 0 to 7, all different within a row; in each aligned block of 128 rows (0 to 127, 128 to 255, ..., all dimensions but the last counted through in order) at most 36 rows name the same one
- second_gates: float32 [4, 8192, 2], P('pipe', ('expert', 'dp')), may hold values from 0.1 to 1
- new_slot: int32 [4, 8], P('pipe'), may hold values from 0 to 7, each once within a row
- inner_weight: float32 [4, 16, 2, 2048, 384], P('pipe', 'expert', None, 'dp'), may hold values from -0.125 to 0.125
- outer_weight: float32 [4, 16, 384, 2048], P('pipe', 'expert', None, 'dp'), may hold values from -0.21875 to 0.21875
- inner_mean: bfloat16 [4, 16, 2, 2048, 384], P('pipe', 'expert', None, 'dp'), may hold values from -60 to 60
- outer_mean: bfloat16 [4, 16, 384, 2048], P('pipe', 'expert', None, 'dp'), may hold values from -60 to 60
- inner_square: bfloat16 [4, 16, 2, 2048, 384], P('pipe', 'expert', None, 'dp'), may hold values from 10 to 1000
- outer_square: bfloat16 [4, 16, 384, 2048], P('pipe', 'expert', None, 'dp'), may hold values from 10 to 1000
Outputs:
- layer_out: bfloat16 [4, 8192, 2048], P('pipe', ('expert', 'dp'))
- weight_inner: float32 [4, 16, 2, 2048, 384], P('pipe', 'expert', None, 'dp')
- weight_outer: float32 [4, 16, 384, 2048], P('pipe', 'expert', None, 'dp')
- mean_inner: bfloat16 [4, 16, 2, 2048, 384], P('pipe', 'expert', None, 'dp')
- mean_outer: bfloat16 [4, 16, 384, 2048], P('pipe', 'expert', None, 'dp')
- square_inner: bfloat16 [4, 16, 2, 2048, 384], P('pipe', 'expert', None, 'dp')
- square_outer: bfloat16 [4, 16, 384, 2048], P('pipe', 'expert', None, 'dp')
Inputs may be any that keep to these rules, and one draw needn't show every extreme that they name: `first_ids`: each token names 2 different experts. Within the rows of one device no expert is named more than 36 times, and some device names some expert exactly 36 times. `second_ids`: as first_ids. `new_slot`: for each section, a permutation of the 8 experts.
All inputs are finite; a program needn't handle non-finite values.
Results may differ from a plain program's by a relative error of at most 0.008.
Values may be sent and summed in bfloat16 or wider, within the bound.
No kernel may reach another device: no remote copies, remote signals or barrier semaphores. Data moves between devices by JAX's collectives and lax.ppermute only.
A program may use at most 128 MiB of HBM per device.

v0:
```python
import jax
import jax.numpy as jnp
from jax import lax
from jax.sharding import PartitionSpec as P

norm_eps = 1e-06
learn_rate = 0.001
beta_one = 0.9
beta_two = 0.95
adam_eps = 1e-08
bias_one = 0.999973438601112
bias_two = 0.994079470779667


def side_by_side(arrays, axis, split_dim, concat_dim, along):
    ends, at = ([], 0)
    for a in arrays[:-1]:
        at += a.shape[along]
        ends.append(at)
    both = jnp.concatenate(arrays, axis=along)
    return tuple(
        jnp.split(
            lax.all_to_all(both, axis, split_axis=split_dim, concat_axis=concat_dim, tiled=True),
            ends,
            axis=along,
        )
    )


def for_sending(array):

    def short(part):
        return part.astype(jnp.bfloat16) if part.dtype == jnp.float32 else part

    return jax.tree.map(short, array)


def cut_along(array, dim, size):
    before, after = (array.shape[:dim], array.shape[dim + 1 :])
    return jnp.moveaxis(array.reshape(*before, size, -1, *after), dim, 0)


def sum_together(arrays, axis, dims):
    size = lax.axis_size(axis)
    parts = [cut_along(a, dim, size) for a, dim in zip(arrays, dims)]
    lines = jnp.concatenate([b.reshape(size, -1) for b in parts], axis=1)
    rows = max(16, -(-lines.shape[1] // 1024) * 8)
    lines = jnp.pad(lines, ((0, 0), (0, rows * 128 - lines.shape[1]))).reshape(-1, 128)
    line, at, outs = (lax.psum_scatter(lines, axis, tiled=True).reshape(-1), 0, [])
    for b in parts:
        part = b[0]
        outs.append(line[at : at + part.size].reshape(part.shape))
        at += part.size
    return tuple(outs)


def passed_along(block, axis, distance):
    devices = range(lax.axis_size(axis))
    route = [((i - distance) % len(devices), i) for i in devices]
    return lax.ppermute(block, axis, route)


def normed(values, gain_row):
    widened = values.astype(jnp.float32)
    inverse_rms = lax.rsqrt(jnp.mean(widened * widened, axis=-1, keepdims=True) + norm_eps)
    return (widened * inverse_rms * gain_row).astype(jnp.bfloat16)


def silu_parts(gate_proj):
    logistic = jax.nn.sigmoid(gate_proj)
    return (gate_proj * logistic, logistic * (1.0 + gate_proj * (1.0 - logistic)))


def half_forward(token_rows, inner_full, outer_full):
    gate_proj = jnp.dot(token_rows, inner_full[0], preferred_element_type=jnp.float32)
    up_proj = jnp.dot(token_rows, inner_full[1], preferred_element_type=jnp.float32)
    activity = (silu_parts(gate_proj)[0] * up_proj).astype(jnp.bfloat16)
    half_out = jnp.dot(activity, outer_full, preferred_element_type=jnp.float32).astype(
        jnp.bfloat16
    )
    return (half_out, activity, gate_proj, up_proj)


def half_backward(token_rows, grad_rows, outer_full, activity, gate_proj, up_proj):
    grad_outer = jnp.dot(activity.T, grad_rows, preferred_element_type=jnp.float32)
    d_active = jnp.dot(grad_rows, outer_full.T, preferred_element_type=jnp.float32)
    swish_value, swish_slope = silu_parts(gate_proj)
    d_gate = (d_active * up_proj * swish_slope).astype(jnp.bfloat16)
    d_upper = (d_active * swish_value).astype(jnp.bfloat16)
    grad_gate = jnp.dot(token_rows.T, d_gate, preferred_element_type=jnp.float32)
    grad_upper = jnp.dot(token_rows.T, d_upper, preferred_element_type=jnp.float32)
    return (jnp.stack([grad_gate, grad_upper]), grad_outer)


def slot_index(ids, pair_of, capacity):
    flattened = ids.reshape(-1)
    expert_row = jnp.arange(pair_of.shape[0], dtype=jnp.int32)
    onehot = (flattened[:, None] == expert_row[None, :]).astype(jnp.int32)
    ranking = jnp.sum((jnp.cumsum(onehot, axis=0) - 1) * onehot, axis=1)
    target = jnp.sum(onehot * pair_of[None, :], axis=1)
    return (target * capacity + ranking).reshape(ids.shape)


def selection(slots, values, total_slots):
    positions = jnp.arange(total_slots, dtype=jnp.int32)
    result = jnp.zeros((total_slots, slots.shape[0]), jnp.float32)
    for column in range(slots.shape[1]):
        result = result + jnp.where(
            slots[:, column][None, :] == positions[:, None], values[:, column][None, :], 0.0
        )
    return result


def both_halves(packed, pair_count, capacity):
    return jnp.repeat(packed.reshape(pair_count, capacity, packed.shape[-1]), 2, axis=0)


def gather_weights(inner_master, outer_master):
    inner_full, outer_full = (
        lax.all_gather(inner_master.astype(jnp.bfloat16), "dp", axis=3, tiled=True),
        lax.all_gather(outer_master.astype(jnp.bfloat16), "dp", axis=3, tiled=True),
    )
    return (inner_full[0, 0], outer_full[0, 0])


def forward_layer(token_rows, gain_row, ids, gates, pair_of, inner_full, outer_full, capacity):
    pair_count = pair_of.shape[0]
    normal = normed(token_rows, gain_row)
    slots = slot_index(ids, pair_of, capacity)
    picker = selection(slots, jnp.ones(slots.shape, jnp.float32), pair_count * capacity).astype(
        jnp.bfloat16
    )
    packed = jnp.dot(picker, normal, preferred_element_type=jnp.float32).astype(jnp.bfloat16)
    send_rows = both_halves(packed, pair_count, capacity)
    arrived = lax.all_to_all(send_rows, "expert", split_axis=0, concat_axis=0, tiled=True)
    shape = arrived.shape
    half_out, activity, gate_proj, up_proj = half_forward(
        arrived.reshape(-1, shape[-1]), inner_full, outer_full
    )
    hidden = activity.shape[-1]
    half_out, arrived, activity, gate_proj, up_proj = (
        half_out.reshape(shape),
        arrived,
        activity.reshape(shape[0], shape[1], hidden),
        gate_proj.reshape(shape[0], shape[1], hidden),
        up_proj.reshape(shape[0], shape[1], hidden),
    )
    returned = lax.all_to_all(half_out, "expert", split_axis=0, concat_axis=0, tiled=True)
    summed = returned.astype(jnp.float32).reshape(pair_count, 2, capacity, -1).sum(axis=1)
    summed = summed.reshape(pair_count * capacity, -1)
    picked = summed[slots]
    mixed_rows = token_rows.astype(jnp.float32) + jnp.sum(gates[..., None] * picked, axis=1)
    return (mixed_rows.astype(jnp.bfloat16), (slots, arrived, activity, gate_proj, up_proj))


def adam_step(weight, mean, square, grads):
    mean_new = (beta_one * mean.astype(jnp.float32) + (1.0 - beta_one) * grads).astype(jnp.bfloat16)
    square_new = (beta_two * square.astype(jnp.float32) + (1.0 - beta_two) * grads * grads).astype(
        jnp.bfloat16
    )
    mean_wide = lax.optimization_barrier(mean_new).astype(jnp.float32)
    square_wide = lax.optimization_barrier(square_new).astype(jnp.float32)
    update = mean_wide / bias_one / (jnp.sqrt(square_wide / bias_two) + adam_eps)
    return (weight - learn_rate * update, mean_new, square_new)


def relocate_master(inner_master, outer_master, source):
    devices = source.shape[0]
    inner_spread, outer_spread = tuple(
        (
            part.astype(jnp.float32)
            for part in side_by_side(
                (
                    inner_master.reshape(devices, -1).astype(jnp.bfloat16),
                    outer_master.reshape(devices, -1).astype(jnp.bfloat16),
                ),
                "expert",
                0,
                0,
                1,
            )
        )
    )
    inner_order = jnp.take(inner_spread, source, axis=0)
    outer_order = jnp.take(outer_spread, source, axis=0)
    inner_back, outer_back = (
        lax.all_to_all(
            for_sending(inner_order), "expert", split_axis=0, concat_axis=0, tiled=True
        ).astype(inner_order.dtype),
        lax.all_to_all(
            for_sending(outer_order), "expert", split_axis=0, concat_axis=0, tiled=True
        ).astype(outer_order.dtype),
    )
    return (inner_back.reshape(inner_master.shape), outer_back.reshape(outer_master.shape))


def relocate_moments(first_inner, first_outer, second_inner, second_outer, source):
    devices = source.shape[0]
    spread = side_by_side(
        (
            first_inner.reshape(devices, -1),
            first_outer.reshape(devices, -1),
            second_inner.reshape(devices, -1),
            second_outer.reshape(devices, -1),
        ),
        "expert",
        0,
        0,
        1,
    )
    ordered = [jnp.take(member, source, axis=0) for member in spread]
    back = side_by_side((ordered[0], ordered[1], ordered[2], ordered[3]), "expert", 0, 0, 1)
    return (
        back[0].reshape(first_inner.shape),
        back[1].reshape(first_outer.shape),
        back[2].reshape(second_inner.shape),
        back[3].reshape(second_outer.shape),
    )


def per_device(
    tokens,
    cotangent,
    norm_gain,
    first_ids,
    first_gates,
    second_ids,
    second_gates,
    new_slot,
    inner_weight,
    outer_weight,
    inner_mean,
    outer_mean,
    inner_square,
    outer_square,
):
    pair_count = new_slot.shape[1]
    rows_here = tokens.shape[1]
    top_count = first_ids.shape[2]
    width = tokens.shape[2]
    usual = rows_here * top_count // pair_count
    capacity = min(rows_here, usual + usual // 8)
    gain_row = norm_gain[0]
    identity_map = jnp.arange(pair_count, dtype=jnp.int32)
    inner_full, outer_full = gather_weights(inner_weight, outer_weight)
    first_out, saved = forward_layer(
        tokens[0],
        gain_row,
        first_ids[0],
        first_gates[0],
        identity_map,
        inner_full,
        outer_full,
        capacity,
    )
    slots, arrived, activity, gate_proj, up_proj = saved
    weighting = selection(slots, first_gates[0], pair_count * capacity)
    grad_packed = jnp.dot(
        weighting, cotangent[0].astype(jnp.float32), precision=lax.Precision.HIGHEST
    ).astype(jnp.bfloat16)
    grad_send = both_halves(grad_packed, pair_count, capacity)
    grad_arrived = lax.all_to_all(grad_send, "expert", split_axis=0, concat_axis=0, tiled=True)
    hidden = activity.shape[-1]
    grad_inner, grad_outer = half_backward(
        arrived.reshape(-1, width),
        grad_arrived.reshape(-1, width),
        outer_full,
        activity.reshape(-1, hidden),
        gate_proj.reshape(-1, hidden),
        up_proj.reshape(-1, hidden),
    )
    sum_inner, sum_outer = tuple(
        (
            part.astype(jnp.float32)
            for part in sum_together(
                (
                    grad_inner[None, None].astype(jnp.bfloat16),
                    grad_outer[None, None].astype(jnp.bfloat16),
                ),
                "dp",
                (3, 3),
            )
        )
    )
    stepped_inner, mean_in_new, square_in_new = adam_step(
        inner_weight, inner_mean, inner_square, sum_inner
    )
    stepped_outer, mean_out_new, square_out_new = adam_step(
        outer_weight, outer_mean, outer_square, sum_outer
    )
    new_pairs = new_slot[0]
    inverse = jnp.sum(
        jnp.where(new_pairs[:, None] == identity_map[None, :], identity_map[:, None], 0), axis=0
    )
    device_ids = jnp.arange(2 * pair_count, dtype=jnp.int32)
    source = 2 * jnp.repeat(inverse, 2) + device_ids % 2
    moved_inner, moved_outer = relocate_master(stepped_inner, stepped_outer, source)
    moved_mean_in, moved_mean_out, moved_square_in, moved_square_out = relocate_moments(
        mean_in_new, mean_out_new, square_in_new, square_out_new, source
    )
    inner_two, outer_two = gather_weights(moved_inner, moved_outer)
    shifted = passed_along(first_out, "pipe", 1)
    second_out, unused = forward_layer(
        shifted, gain_row, second_ids[0], second_gates[0], new_pairs, inner_two, outer_two, capacity
    )
    return (
        second_out[None],
        moved_inner,
        moved_outer,
        moved_mean_in,
        moved_mean_out,
        moved_square_in,
        moved_square_out,
    )


def solution(mesh):
    return jax.shard_map(
        per_device,
        mesh=mesh,
        in_specs=(
            P("pipe", ("expert", "dp"), None),
            P("pipe", ("expert", "dp"), None),
            P("pipe", None),
            P("pipe", ("expert", "dp"), None),
            P("pipe", ("expert", "dp"), None),
            P("pipe", ("expert", "dp"), None),
            P("pipe", ("expert", "dp"), None),
            P("pipe", None),
            P("pipe", "expert", None, "dp", None),
            P("pipe", "expert", None, "dp"),
            P("pipe", "expert", None, "dp", None),
            P("pipe", "expert", None, "dp"),
            P("pipe", "expert", None, "dp", None),
            P("pipe", "expert", None, "dp"),
        ),
        out_specs=(
            P("pipe", ("expert", "dp"), None),
            P("pipe", "expert", None, "dp", None),
            P("pipe", "expert", None, "dp"),
            P("pipe", "expert", None, "dp", None),
            P("pipe", "expert", None, "dp"),
            P("pipe", "expert", None, "dp", None),
            P("pipe", "expert", None, "dp"),
        ),
        check_vma=False,
    )
```

profile of v0, /device:TPU:1, one launch (start us, length us, event | category | flops | bytes accessed | tf_op | source)
XLA Modules:
  0.0 659.8 jit_solution(6963974720981108128)
XLA Ops:
  14.6 10.1 %all-to-all-start = ((bf16[16,36,2048]{2,1,0:T(8,128)(2,1)}), bf16[16,36,2048]{2,1,0:T(8,128)(2,1)S(1)}, u32[]{:S(2)}, u32[]{:S(2)}) async-start(bf16[16,36,2048]{2,1,0:T(8,128)(2,1)} %bitcast.153), calls=%async_computation | async-start | bytes 5242880 | tf_op jit(solution)/shard_map/all_to_all | solution.py:135
  31.1 53.4 %all-to-all-done = bf16[16,36,2048]{2,1,0:T(8,128)(2,1)S(1)} async-done(((bf16[16,36,2048]{2,1,0:T(8,128)(2,1)}), bf16[16,36,2048]{2,1,0:T(8,128)(2,1)S(1)}, u32[]{:S(2)}, u32[]{:S(2)}) %all-to-all-start) | async-done | bytes 2359328 | tf_op jit(solution)/shard_map/all_to_all | solution.py:135
  87.6 5.4 all-to-all-start.3
  98.2 54.7 %all-to-all-done.3 = bf16[16,36,2048]{2,1,0:T(8,128)(2,1)} async-done(((bf16[16,36,2048]{2,1,0:T(8,128)(2,1)}), bf16[16,36,2048]{2,1,0:T(8,128)(2,1)}, u32[]{:S(2)}, u32[]{:S(2)}) %all-to-all-start.3) | async-done | bytes 2359328 | tf_op jit(solution)/shard_map/all_to_all | solution.py:262
  170.5 4.7 reshape.547
  180.7 20.7 %pad_maximum_fusion = bf16[4,589824]{1,0:T(4,128)(2,1)} fusion(bf16[4,196608]{1,0:T(4,128)(2,1)S(1)} %bitcast.159, bf16[4,393216]{1,0:T(4,128)(2,1)} %reshape.547), kind=kLoop, calls=%fused_computation.10 | loop fusion | flops 9437184 | bytes 9437184 | tf_op jit(solution)/shard_map/concatenate | solution.py:46
  201.4 9.2 %reshape.550 = bf16[18432,128]{1,0:T(8,128)(2,1)} reshape(bf16[4,589824]{1,0:T(4,128)(2,1)} %pad_maximum_fusion) | data formatting | bytes 9437184 | tf_op jit(solution)/shard_map/reshape | solution.py:48
  215.6 5.4 all-to-all-start.1
  221.0 42.7 %reduce-scatter.2.cloned.1.call-done = bf16[4608,128]{1,0:T(8,128)(2,1)} async-done(((bf16[18432,128]{1,0:T(8,128)(2,1)}), bf16[4608,128]{1,0:T(8,128)(2,1)}) %reduce-scatter.2.cloned.1.call-update) | async-done | bytes 1179664 | tf_op jit(solution)/shard_map/reduce_scatter | solution.py:49
  293.9 8.2 %all-to-all-start.4 = ((bf16[16,2,18432]{2,1,0:T(2,128)(2,1)}), bf16[16,2,18432]{2,1,0:T(2,128)(2,1)}, u32[]{:S(2)}, u32[]{:S(2)}) async-start(bf16[16,2,18432]{2,1,0:T(2,128)(2,1)} %reshape.658), calls=%async_computation.5 | async-start | bytes 2359296 | tf_op jit(solution)/shard_map/all_to_all | solution.py:23
  321.5 11.1 %all-to-all-done.4 = bf16[16,2,18432]{2,1,0:T(2,128)(2,1)} async-done(((bf16[16,2,18432]{2,1,0:T(2,128)(2,1)}), bf16[16,2,18432]{2,1,0:T(2,128)(2,1)}, u32[]{:S(2)}, u32[]{:S(2)}) %all-to-all-start.4) | async-done | bytes 1179680 | tf_op jit(solution)/shard_map/all_to_all | solution.py:23
  332.6 4.4 reshape.659
  356.5 13.4 %all-to-all-done.5 = bf16[16,2,12288]{2,1,0:T(2,128)(2,1)} async-done(((bf16[16,2,12288]{2,1,0:T(2,128)(2,1)}), bf16[16,2,12288]{2,1,0:T(2,128)(2,1)}, u32[]{:S(2)}, u32[]{:S(2)}) %all-to-all-start.5) | async-done | bytes 786464 | tf_op jit(solution)/shard_map/all_to_all | solution.py:187
  373.8 4.8 multiply_reduce_fusion.1
  380.5 13.4 %collective-permute-done = bf16[128,2048]{1,0:T(8,128)(2,1)S(1)} collective-permute-done((bf16[128,2048]{1,0:T(8,128)(2,1)S(1)}, bf16[128,2048]{1,0:T(8,128)(2,1)S(1)}, u32[]{:S(2)}, u32[]{:S(2)}) %collective-permute-start) | collective-permute-done | bytes 524320 | tf_op jit(solution)/shard_map/ppermute | solution.py:60
  403.6 5.2 reshape.663
  408.8 6.9 %reduce.6 = bf16[16,24576]{1,0:T(8,128)(2,1)} reduce(bf16[16,1,24576]{2,1,0:T(2,128)(2,1)} %reshape.663, bf16[]{:T(256)} %constant.144), dimensions={1}, to_apply=%all_to_all.58.reduce_sub_computation | reduce | bytes 1572866 | tf_op jit(solution)/shard_map/all_to_all | solution.py:187
  418.1 9.3 %all-to-all-done.8 = bf16[16,2,36864]{2,1,0:T(2,128)(2,1)S(1)} async-done(((bf16[16,2,36864]{2,1,0:T(2,128)(2,1)}), bf16[16,2,36864]{2,1,0:T(2,128)(2,1)S(1)}, u32[]{:S(2)}, u32[]{:S(2)}) %all-to-all-start.8) | async-done | bytes 2359328 | tf_op jit(solution)/shard_map/all_to_all | solution.py:23
  430.7 5.5 all-to-all-start.2
  436.2 7.0 %reshape.665 = bf16[16,1,73728]{2,1,0:T(2,128)(2,1)} reshape(bf16[16,2,36864]{2,1,0:T(2,128)(2,1)S(1)} %all-to-all-done.8) | data formatting | bytes 4718592
  443.2 5.0 copy.105
  454.3 41.7 %all-to-all-done.2 = bf16[16,36,2048]{2,1,0:T(8,128)(2,1)} async-done(((bf16[16,36,2048]{2,1,0:T(8,128)(2,1)}), bf16[16,36,2048]{2,1,0:T(8,128)(2,1)}, u32[]{:S(2)}, u32[]{:S(2)}) %all-to-all-start.2) | async-done | bytes 2359328 | tf_op jit(solution)/shard_map/all_to_all | solution.py:135
  495.9 5.4 all-to-all-start.6
  510.3 5.6 all-to-all-done.6
  534.0 4.5 fusion.15
  538.6 14.7 %all-gather.11.cloned.1.call-done = bf16[1,1,384,2048]{3,2,1,0:T(8,128)(2,1)} async-done(((bf16[1,1,384,512]{3,2,1,0:T(8,128)(2,1)}), bf16[1,1,384,2048]{3,2,1,0:T(8,128)(2,1)}) %all-gather.11.cloned.1.call-update) | async-done | bytes 1572880 | tf_op jit(solution)/shard_map/all_gather | solution.py:121
  553.2 6.9 %convolution_convert_fusion = bf16[576,2048]{1,0:T(8,128)(2,1)} fusion(bf16[1,1,384,2048]{3,2,1,0:T(8,128)(2,1)} %all-gather.11.cloned.1.call-done, bf16[576,2048]{1,0:T(8,128)(2,1)} %reshape.542, bf16[1,1,2,2048,384]{4,3,2,1,0:T(8,128)(2,1)} %all-gather.9.cloned.1.call-done, f32[576,384]{1,0:T(8,128)} %fusion.15), kind=kOutput, calls=%fused_computation.12 | convolution fusion | flops 1814446080 | bytes 8749056 | tf_op jit(solution)/shard_map/dot_general | solution.py:78
  564.3 8.8 %all-to-all-done.9 = bf16[16,2,36864]{2,1,0:T(2,128)(2,1)S(1)} async-done(((bf16[16,2,36864]{2,1,0:T(2,128)(2,1)}), bf16[16,2,36864]{2,1,0:T(2,128)(2,1)S(1)}, u32[]{:S(2)}, u32[]{:S(2)}) %all-to-all-start.9) | async-done | bytes 2359328 | tf_op jit(solution)/shard_map/all_to_all | solution.py:23
  574.5 5.5 all-to-all-start.7
  580.0 10.7 %reshape.667 = bf16[16,1,73728]{2,1,0:T(2,128)(2,1)} reshape(bf16[16,2,36864]{2,1,0:T(2,128)(2,1)} %copy-done.2) | data formatting | bytes 4718592
  590.7 4.9 copy.104
  606.1 33.7 %all-to-all-done.7 = bf16[16,36,2048]{2,1,0:T(8,128)(2,1)S(1)} async-done(((bf16[16,36,2048]{2,1,0:T(8,128)(2,1)}), bf16[16,36,2048]{2,1,0:T(8,128)(2,1)S(1)}, u32[]{:S(2)}, u32[]{:S(2)}) %all-to-all-start.7) | async-done | bytes 2359328 | tf_op jit(solution)/shard_map/all_to_all | solution.py:148
  (223 shorter events, 202.3 us)
Async XLA Ops:
  7.2 19.5 %copy-start = (bf16[1,128,2048]{2,1,0:T(8,128)(2,1)S(1)}, bf16[1,128,2048]{2,1,0:T(8,128)(2,1)}, u32[]{:S(2)}) copy-start(bf16[1,128,2048]{2,1,0:T(8,128)(2,1)} %param.19) | copy-start | bytes 1572868
  14.6 12.1 %copy-start.24 = (f32[1,128,2]{1,2,0:T(2,128)S(1)}, f32[1,128,2]{1,2,0:T(2,128)}, u32[]{:S(2)}) copy-start(f32[1,128,2]{1,2,0:T(2,128)} %param.22) | copy-start | bytes 3076
  14.6 69.9 %all-to-all-start = ((bf16[16,36,2048]{2,1,0:T(8,128)(2,1)}), bf16[16,36,2048]{2,1,0:T(8,128)(2,1)S(1)}, u32[]{:S(2)}, u32[]{:S(2)}) async-start(bf16[16,36,2048]{2,1,0:T(8,128)(2,1)} %bitcast.153), calls=%async_computation | async-start | bytes 5242880 | tf_op jit(solution)/shard_map/all_to_all | solution.py:135
  24.7 130.9 %all-gather.7.cloned.1.call-start = ((), (), s32[]{:S(2)}) async-start(), calls=%async_computation.12 | async-start | bytes 1966080 | tf_op jit(solution)/shard_map/all_gather | solution.py:121
  87.6 65.3 %all-to-all-start.3 = ((bf16[16,36,2048]{2,1,0:T(8,128)(2,1)}), bf16[16,36,2048]{2,1,0:T(8,128)(2,1)}, u32[]{:S(2)}, u32[]{:S(2)}) async-start(bf16[16,36,2048]{2,1,0:T(8,128)(2,1)} %bitcast.154), calls=%async_computation.3 | async-start | bytes 5242880 | tf_op jit(solution)/shard_map/all_to_all | solution.py:262
  93.0 66.3 %all-gather.5.cloned.1.call-start = ((), (), s32[]{:S(2)}) async-start(), calls=%async_computation.11 | async-start | bytes 3932160 | tf_op jit(solution)/shard_map/all_gather | solution.py:120
  95.5 168.2 %reduce-scatter.2.cloned.1.call-start = ((), (), s32[]{:S(2)}) async-start(), calls=%async_computation.13 | async-start | bytes 5898240 | tf_op jit(solution)/shard_map/reduce_scatter | solution.py:49
  215.6 78.3 %all-to-all-start.1 = ((bf16[16,36,2048]{2,1,0:T(8,128)(2,1)}), bf16[16,36,2048]{2,1,0:T(8,128)(2,1)S(1)}, u32[]{:S(2)}, u32[]{:S(2)}) async-start(bf16[16,36,2048]{2,1,0:T(8,128)(2,1)} %reshape.535), calls=%async_computation.1 | async-start | bytes 5242880 | tf_op jit(solution)/shard_map/all_to_all | solution.py:148
  291.1 11.0 %copy-start.27 = (s32[1,8]{1,0:T(1,128)S(1)}, s32[1,8]{1,0:T(1,128)}, u32[]{:S(2)}) copy-start(s32[1,8]{1,0:T(1,128)} %param.25) | copy-start | bytes 100
  291.1 12.8 %copy-start.25 = (s32[1,128,2]{1,2,0:T(2,128)S(1)}, s32[1,128,2]{1,2,0:T(2,128)}, u32[]{:S(2)}) copy-start(s32[1,128,2]{1,2,0:T(2,128)} %param.23) | copy-start | bytes 3076
  293.9 38.7 %all-to-all-start.4 = ((bf16[16,2,18432]{2,1,0:T(2,128)(2,1)}), bf16[16,2,18432]{2,1,0:T(2,128)(2,1)}, u32[]{:S(2)}, u32[]{:S(2)}) async-start(bf16[16,2,18432]{2,1,0:T(2,128)(2,1)} %reshape.658), calls=%async_computation.5 | async-start | bytes 2359296 | tf_op jit(solution)/shard_map/all_to_all | solution.py:23
  314.3 4.8 copy-start.5
  340.7 6.9 %copy-start.16 = (bf16[16,12288]{1,0:T(8,128)(2,1)S(1)}, bf16[16,12288]{1,0:T(8,128)(2,1)}, u32[]{:S(2)}) copy-start(bf16[16,12288]{1,0:T(8,128)(2,1)} %reshape.556) | copy-start | bytes 1179652
  343.4 26.5 %all-to-all-start.5 = ((bf16[16,2,12288]{2,1,0:T(2,128)(2,1)}), bf16[16,2,12288]{2,1,0:T(2,128)(2,1)}, u32[]{:S(2)}, u32[]{:S(2)}) async-start(bf16[16,2,12288]{2,1,0:T(2,128)(2,1)} %reshape.662), calls=%async_computation.6 | async-start | bytes 1572864 | tf_op jit(solution)/shard_map/all_to_all | solution.py:187
  356.5 17.3 %copy-start.19 = (f32[128,2]{1,0:T(8,128)S(1)}, f32[128,2]{1,0:T(8,128)}, u32[]{:S(2)}) copy-start(f32[128,2]{1,0:T(8,128)} %copy.67) | copy-start | bytes 3076
  369.9 57.5 %all-to-all-start.8 = ((bf16[16,2,36864]{2,1,0:T(2,128)(2,1)}), bf16[16,2,36864]{2,1,0:T(2,128)(2,1)S(1)}, u32[]{:S(2)}, u32[]{:S(2)}) async-start(bf16[16,2,36864]{2,1,0:T(2,128)(2,1)} %reshape.664), calls=%async_computation.9 | async-start | bytes 4718592 | tf_op jit(solution)/shard_map/all_to_all | solution.py:23
  373.5 5.1 copy-start.10
  373.5 6.5 slice-start
  373.5 6.5 copy-start.23
  373.5 6.5 copy-start.28
  373.5 6.7 %copy-start.29 = (s32[16]{0:T(128)S(1)}, s32[16]{0:T(128)}, u32[]{:S(2)}) copy-start(s32[16]{0:T(128)} %get-tuple-element.18) | copy-start | bytes 196
  373.6 20.5 %copy-start.21 = (f32[1,2048]{1,0:T(1,128)S(1)}, f32[1,2048]{1,0:T(1,128)}, u32[]{:S(2)}) copy-start(f32[1,2048]{1,0:T(1,128)} %param.20) | copy-start | bytes 24580
  373.6 160.5 %all-gather.9.cloned.1.call-start = ((), (), s32[]{:S(2)}) async-start(), calls=%async_computation.14 | async-start | bytes 3932160 | tf_op jit(solution)/shard_map/all_gather | solution.py:120
  378.8 15.1 %collective-permute-start = (bf16[128,2048]{1,0:T(8,128)(2,1)S(1)}, bf16[128,2048]{1,0:T(8,128)(2,1)S(1)}, u32[]{:S(2)}, u32[]{:S(2)}) collective-permute-start(bf16[128,2048]{1,0:T(8,128)(2,1)S(1)} %fusion.38), channel_id=1, source_target_pairs={{192,0},{0,64},{64,128},{128,192},{193,1},{1,65},{65,129},{129,193... | collective-permute-start | bytes 1572872 | tf_op jit(solution)/shard_map/ppermute | solution.py:60
  430.7 65.3 %all-to-all-start.2 = ((bf16[16,36,2048]{2,1,0:T(8,128)(2,1)}), bf16[16,36,2048]{2,1,0:T(8,128)(2,1)}, u32[]{:S(2)}, u32[]{:S(2)}) async-start(bf16[16,36,2048]{2,1,0:T(8,128)(2,1)} %bitcast.15), calls=%async_computation.2 | async-start | bytes 5242880 | tf_op jit(solution)/shard_map/all_to_all | solution.py:135
  495.9 19.9 %all-to-all-start.6 = ((bf16[16,2,6144]{2,1,0:T(2,128)(2,1)}), bf16[16,2,6144]{2,1,0:T(2,128)(2,1)S(1)}, u32[]{:S(2)}, u32[]{:S(2)}) async-start(bf16[16,2,6144]{2,1,0:T(2,128)(2,1)} %reshape.660), calls=%async_computation.7 | async-start | bytes 786432 | tf_op jit(solution)/shard_map/all_to_all | solution.py:190
  515.9 57.1 %all-to-all-start.9 = ((bf16[16,2,36864]{2,1,0:T(2,128)(2,1)}), bf16[16,2,36864]{2,1,0:T(2,128)(2,1)S(1)}, u32[]{:S(2)}, u32[]{:S(2)}) async-start(bf16[16,2,36864]{2,1,0:T(2,128)(2,1)} %reshape.666), calls=%async_computation.10 | async-start | bytes 4718592 | tf_op jit(solution)/shard_map/all_to_all | solution.py:23
  519.5 6.3 copy-start.26
  519.5 33.7 %all-gather.11.cloned.1.call-start = ((), (), s32[]{:S(2)}) async-start(), calls=%async_computation.15 | async-start | bytes 1966080 | tf_op jit(solution)/shard_map/all_gather | solution.py:121
  526.5 4.1 copy-start.13
  574.5 65.2 %all-to-all-start.7 = ((bf16[16,36,2048]{2,1,0:T(8,128)(2,1)}), bf16[16,36,2048]{2,1,0:T(8,128)(2,1)S(1)}, u32[]{:S(2)}, u32[]{:S(2)}) async-start(bf16[16,36,2048]{2,1,0:T(8,128)(2,1)} %reshape.551), calls=%async_computation.8 | async-start | bytes 5242880 | tf_op jit(solution)/shard_map/all_to_all | solution.py:148
  646.4 6.7 %copy-start.1 = (bf16[1,128,2048]{2,1,0:T(8,128)(2,1)S(1)}, bf16[1,128,2048]{2,1,0:T(8,128)(2,1)}, u32[]{:S(2)}) copy-start(bf16[1,128,2048]{2,1,0:T(8,128)(2,1)} %param.19) | copy-start | bytes 1572868
  (17 other events, 39.5 us)
Sparse Core Ops, SparseCore 0:
  27.9 30.1 all-gather.6
  96.2 43.1 all-gather.4
  210.7 52.8 reduce-scatter.1
  418.2 39.8 all-gather.8
  525.6 27.5 all-gather.10
where the time goes:
time: 666 us; the launch traced here: 660 us
  waiting for transfers between devices  302 us (45%)
  local copies, waits for them, and re-layouts  160 us (24%)
  other arithmetic  88.4 us (13%)
  starting transfers between devices  59.5 us (9%)
  matrix products  34.5 us (5%)
  between operations  14.7 us (2%)
    all_to_all x2, waiting for transfers between devices, forward_layer(): lax.all_to_all(send_rows, 'expert', split_axis=0, concat_axis=0, tiled=True)  95.1 us
    unnamed x79, local copies, waits for them, and re-layouts  60 us
    all_to_all x1, waiting for transfers between devices, per_device(): lax.all_to_all(grad_send, 'expert', split_axis=0, concat_axis=0, tiled=True)  54.7 us
    reduce_scatter x1, waiting for transfers between devices, sum_together(): lax.psum_scatter(lines, axis, tiled=True).reshape(-1)  42.7 us
    all_to_all x2, waiting for transfers between devices, forward_layer(): lax.all_to_all(half_out, 'expert', split_axis=0, concat_axis=0, tiled=True)  33.7 us
    all_to_all x3, waiting for transfers between devices, side_by_side(): lax.all_to_all(both, axis, split_axis=split_dim, concat_axis=concat_dim,...  29.2 us
    concatenate x1, other arithmetic, sum_together(): lines = jnp.concatenate([b.reshape(size, -1) for b in parts], axis=1)  20.7 us
    all_to_all x2, starting transfers between devices, forward_layer(): lax.all_to_all(send_rows, 'expert', split_axis=0, concat_axis=0, tiled=True)  15.6 us
  transfers between devices with their start and end apart: 16, of which 12 were waited for; matrix products, arithmetic and copies ran while one was open for 29% of the time, Pallas kernels for 0%

commit v1 on v0

--- a/solution.py
+++ b/solution.py
@@ -10,6 +10,11 @@
 adam_eps = 1e-08
 bias_one = 0.999973438601112
 bias_two = 0.994079470779667
+
+
+def swapped_in(array, mesh_axis, d):
+    sent = jnp.stack([array] * lax.axis_size(mesh_axis))
+    return jnp.concatenate(lax.all_to_all(sent, mesh_axis, 0, 0), axis=d)
 
 
 def side_by_side(arrays, axis, split_dim, concat_dim, along):
@@ -118,7 +123,7 @@
 def gather_weights(inner_master, outer_master):
     inner_full, outer_full = (
         lax.all_gather(inner_master.astype(jnp.bfloat16), "dp", axis=3, tiled=True),
-        lax.all_gather(outer_master.astype(jnp.bfloat16), "dp", axis=3, tiled=True),
+        swapped_in(outer_master.astype(jnp.bfloat16), "dp", 3),
     )
     return (inner_full[0, 0], outer_full[0, 0])
 

time: 666 us -> 763 us (1.15)
  waiting for transfers between devices: 302 us -> 395 us
  starting transfers between devices: 59.5 us -> 70.3 us
    all_to_all x2, waiting for transfers between devices: 33.7 us -> 79.2 us  [forward_layer(): lax.all_to_all(half_out, 'expert', split_axis=0, concat_axis=0, tiled=True)]
    all_to_all x0 -> x2, waiting for transfers between devices: none -> 25.9 us  [swapped_in(): return jnp.concatenate(lax.all_to_all(sent, mesh_axis, 0, 0), axis=d)]
    all_to_all x3, waiting for transfers between devices: 29.2 us -> 50.5 us  [side_by_side(): lax.all_to_all(both, axis, split_axis=split_dim, concat_axis=concat_dim,...]
    all_gather x2 -> x0, waiting for transfers between devices: 14.7 us -> none  [gather_weights(): lax.all_gather(outer_master.astype(jnp.bfloat16), 'dp', axis=3, tiled=True)]
    reduce_scatter x1, waiting for transfers between devices: 42.7 us -> 52.6 us  [sum_together(): lax.psum_scatter(lines, axis, tiled=True).reshape(-1)]
    all_to_all x0 -> x2, starting transfers between devices: none -> 8.71 us  [swapped_in(): return jnp.concatenate(lax.all_to_all(sent, mesh_axis, 0, 0), axis=d)]
  transfers between devices with their start and end apart: 16 -> 16, of which waited for: 12 -> 14; matrix products, arithmetic and copies ran while one was open for 29% -> 23% of each run, Pallas kernels for 0% -> 0%
where the time goes in v1:
time: 763 us; the launch traced here: 756 us
  waiting for transfers between devices  395 us (52%)
  local copies, waits for them, and re-layouts  159 us (21%)
  other arithmetic  81.4 us (11%)
  starting transfers between devices  70.3 us (9%)
  matrix products  34.9 us (5%)
  between operations  14.7 us (2%)
    all_to_all x2, waiting for transfers between devices, forward_layer(): lax.all_to_all(send_rows, 'expert', split_axis=0, concat_axis=0, tiled=True)  93.4 us
    all_to_all x2, waiting for transfers between devices, forward_layer(): lax.all_to_all(half_out, 'expert', split_axis=0, concat_axis=0, tiled=True)  79.2 us
    unnamed x79, local copies, waits for them, and re-layouts  62.1 us
    all_to_all x1, waiting for transfers between devices, per_device(): lax.all_to_all(grad_send, 'expert', split_axis=0, concat_axis=0, tiled=True)  56 us
    reduce_scatter x1, waiting for transfers between devices, sum_together(): lax.psum_scatter(lines, axis, tiled=True).reshape(-1)  52.6 us
    all_to_all x3, waiting for transfers between devices, side_by_side(): lax.all_to_all(both, axis, split_axis=split_dim, concat_axis=concat_dim,...  50.5 us
    all_to_all x2, waiting for transfers between devices, swapped_in(): return jnp.concatenate(lax.all_to_all(sent, mesh_axis, 0, 0), axis=d)  25.9 us
    concatenate x1, other arithmetic, sum_together(): lines = jnp.concatenate([b.reshape(size, -1) for b in parts], axis=1)  20.7 us
  transfers between devices with their start and end apart: 16, of which 14 were waited for; matrix products, arithmetic and copies ran while one was open for 23% of the time, Pallas kernels for 0%

profile of v1, /device:TPU:1, one launch (start us, length us, event | category | flops | bytes accessed | tf_op | source)
XLA Modules:
  0.0 755.9 jit_solution(11903421978836915751)
XLA Ops:
  14.6 10.1 %all-to-all-start = ((bf16[16,36,2048]{2,1,0:T(8,128)(2,1)}), bf16[16,36,2048]{2,1,0:T(8,128)(2,1)S(1)}, u32[]{:S(2)}, u32[]{:S(2)}) async-start(bf16[16,36,2048]{2,1,0:T(8,128)(2,1)} %bitcast.161), calls=%async_computation | async-start | bytes 5242880 | tf_op jit(solution)/shard_map/all_to_all | solution.py:140
  29.1 55.4 %all-to-all-done = bf16[16,36,2048]{2,1,0:T(8,128)(2,1)S(1)} async-done(((bf16[16,36,2048]{2,1,0:T(8,128)(2,1)}), bf16[16,36,2048]{2,1,0:T(8,128)(2,1)S(1)}, u32[]{:S(2)}, u32[]{:S(2)}) %all-to-all-start) | async-done | bytes 2359328 | tf_op jit(solution)/shard_map/all_to_all | solution.py:140
  87.6 5.4 all-to-all-start.4
  96.9 56.0 %all-to-all-done.4 = bf16[16,36,2048]{2,1,0:T(8,128)(2,1)} async-done(((bf16[16,36,2048]{2,1,0:T(8,128)(2,1)}), bf16[16,36,2048]{2,1,0:T(8,128)(2,1)}, u32[]{:S(2)}, u32[]{:S(2)}) %all-to-all-start.4) | async-done | bytes 2359328 | tf_op jit(solution)/shard_map/all_to_all | solution.py:267
  163.5 14.8 %all-to-all-done.1 = bf16[4,1,1,384,512]{3,4,2,1,0:T(8,128)(2,1)} async-done(((bf16[4,1,1,384,512]{3,4,2,1,0:T(8,128)(2,1)}), bf16[4,1,1,384,512]{3,4,2,1,0:T(8,128)(2,1)}, u32[]{:S(2)}, u32[]{:S(2)}) %all-to-all-start.1) | async-done | bytes 1572896 | tf_op jit(solution)/shard_map/all_to_all | solution.py:17
  193.2 4.7 reshape.564
  203.3 20.7 %pad_maximum_fusion = bf16[4,589824]{1,0:T(4,128)(2,1)} fusion(bf16[4,196608]{1,0:T(4,128)(2,1)S(1)} %bitcast.166, bf16[4,393216]{1,0:T(4,128)(2,1)} %reshape.564), kind=kLoop, calls=%fused_computation.10 | loop fusion | flops 9437184 | bytes 9437184 | tf_op jit(solution)/shard_map/concatenate | solution.py:51
  224.0 9.2 %reshape.567 = bf16[18432,128]{1,0:T(8,128)(2,1)} reshape(bf16[4,589824]{1,0:T(4,128)(2,1)} %pad_maximum_fusion) | data formatting | bytes 9437184 | tf_op jit(solution)/shard_map/reshape | solution.py:53
  233.3 52.6 %reduce-scatter.2.cloned.1.call-done = bf16[4608,128]{1,0:T(8,128)(2,1)} async-done(((bf16[18432,128]{1,0:T(8,128)(2,1)}), bf16[4608,128]{1,0:T(8,128)(2,1)}) %reduce-scatter.2.cloned.1.call-update) | async-done | bytes 1179664 | tf_op jit(solution)/shard_map/reduce_scatter | solution.py:54
  307.5 7.6 %all-to-all-start.5 = ((bf16[16,2,18432]{2,1,0:T(2,128)(2,1)}), bf16[16,2,18432]{2,1,0:T(2,128)(2,1)S(1)}, u32[]{:S(2)}, u32[]{:S(2)}) async-start(bf16[16,2,18432]{2,1,0:T(2,128)(2,1)} %reshape.678), calls=%async_computation.6 | async-start | bytes 2359296 | tf_op jit(solution)/shard_map/all_to_all | solution.py:28
  323.7 22.1 %all-to-all-done.5 = bf16[16,2,18432]{2,1,0:T(2,128)(2,1)S(1)} async-done(((bf16[16,2,18432]{2,1,0:T(2,128)(2,1)}), bf16[16,2,18432]{2,1,0:T(2,128)(2,1)S(1)}, u32[]{:S(2)}, u32[]{:S(2)}) %all-to-all-start.5) | async-done | bytes 1179680 | tf_op jit(solution)/shard_map/all_to_all | solution.py:28
  346.7 4.8 all-to-all-start.2
  355.5 4.4 reshape.679
  365.2 45.5 %all-to-all-done.2 = bf16[16,36,2048]{2,1,0:T(8,128)(2,1)} async-done(((bf16[16,36,2048]{2,1,0:T(8,128)(2,1)}), bf16[16,36,2048]{2,1,0:T(8,128)(2,1)}, u32[]{:S(2)}, u32[]{:S(2)}) %all-to-all-start.2) | async-done | bytes 2359328 | tf_op jit(solution)/shard_map/all_to_all | solution.py:153
  410.7 5.5 all-to-all-start.7
  419.0 11.7 %all-to-all-done.7 = bf16[16,2,6144]{2,1,0:T(2,128)(2,1)S(1)} async-done(((bf16[16,2,6144]{2,1,0:T(2,128)(2,1)}), bf16[16,2,6144]{2,1,0:T(2,128)(2,1)S(1)}, u32[]{:S(2)}, u32[]{:S(2)}) %all-to-all-start.7) | async-done | bytes 393248 | tf_op jit(solution)/shard_map/all_to_all | solution.py:195
  444.5 12.9 %all-to-all-done.6 = bf16[16,2,12288]{2,1,0:T(2,128)(2,1)} async-done(((bf16[16,2,12288]{2,1,0:T(2,128)(2,1)}), bf16[16,2,12288]{2,1,0:T(2,128)(2,1)}, u32[]{:S(2)}, u32[]{:S(2)}) %all-to-all-start.6) | async-done | bytes 786464 | tf_op jit(solution)/shard_map/all_to_all | solution.py:192
  479.8 13.2 %collective-permute-done = bf16[128,2048]{1,0:T(8,128)(2,1)S(1)} collective-permute-done((bf16[128,2048]{1,0:T(8,128)(2,1)S(1)}, bf16[128,2048]{1,0:T(8,128)(2,1)S(1)}, u32[]{:S(2)}, u32[]{:S(2)}) %collective-permute-start) | collective-permute-done | bytes 524320 | tf_op jit(solution)/shard_map/ppermute | solution.py:65
  503.4 5.6 reduce.6
  516.9 5.8 all-to-all-start.3
  522.7 10.7 %reshape.685 = bf16[16,1,73728]{2,1,0:T(2,128)(2,1)} reshape(bf16[16,2,36864]{2,1,0:T(2,128)(2,1)} %all-to-all-done.10) | data formatting | bytes 4718592
  533.4 4.9 copy.121
  544.5 37.9 %all-to-all-done.3 = bf16[16,36,2048]{2,1,0:T(8,128)(2,1)} async-done(((bf16[16,36,2048]{2,1,0:T(8,128)(2,1)}), bf16[16,36,2048]{2,1,0:T(8,128)(2,1)}, u32[]{:S(2)}, u32[]{:S(2)}) %all-to-all-start.3) | async-done | bytes 2359328 | tf_op jit(solution)/shard_map/all_to_all | solution.py:140
  597.0 11.1 %all-to-all-done.8 = bf16[4,1,1,384,512]{3,4,2,1,0:T(8,128)(2,1)} async-done(((bf16[4,1,1,384,512]{3,4,2,1,0:T(8,128)(2,1)}), bf16[4,1,1,384,512]{3,4,2,1,0:T(8,128)(2,1)}, u32[]{:S(2)}, u32[]{:S(2)}) %all-to-all-start.8) | async-done | bytes 1572896 | tf_op jit(solution)/shard_map/all_to_all | solution.py:17
  608.1 6.8 all-to-all-start.11
  628.7 4.4 fusion.15
  633.2 6.9 convolution_convert_fusion
  644.2 25.0 %all-to-all-done.11 = bf16[16,2,36864]{2,1,0:T(2,128)(2,1)S(1)} async-done(((bf16[16,2,36864]{2,1,0:T(2,128)(2,1)}), bf16[16,2,36864]{2,1,0:T(2,128)(2,1)S(1)}, u32[]{:S(2)}, u32[]{:S(2)}) %all-to-all-start.11) | async-done | bytes 2359328 | tf_op jit(solution)/shard_map/all_to_all | solution.py:28
  670.6 5.5 all-to-all-start.9
  676.2 10.7 %reshape.687 = bf16[16,1,73728]{2,1,0:T(2,128)(2,1)} reshape(bf16[16,2,36864]{2,1,0:T(2,128)(2,1)} %copy-done.2) | data formatting | bytes 4718592
  686.9 4.9 copy.120
  702.2 33.7 %all-to-all-done.9 = bf16[16,36,2048]{2,1,0:T(8,128)(2,1)S(1)} async-done(((bf16[16,36,2048]{2,1,0:T(8,128)(2,1)}), bf16[16,36,2048]{2,1,0:T(8,128)(2,1)S(1)}, u32[]{:S(2)}, u32[]{:S(2)}) %all-to-all-start.9) | async-done | bytes 2359328 | tf_op jit(solution)/shard_map/all_to_all | solution.py:153
  (226 shorter events, 210.7 us)
Async XLA Ops:
  7.2 17.5 %copy-start = (bf16[1,128,2048]{2,1,0:T(8,128)(2,1)S(1)}, bf16[1,128,2048]{2,1,0:T(8,128)(2,1)}, u32[]{:S(2)}) copy-start(bf16[1,128,2048]{2,1,0:T(8,128)(2,1)} %param.19) | copy-start | bytes 1572868
  14.6 10.1 %copy-start.26 = (f32[1,128,2]{1,2,0:T(2,128)S(1)}, f32[1,128,2]{1,2,0:T(2,128)}, u32[]{:S(2)}) copy-start(f32[1,128,2]{1,2,0:T(2,128)} %param.22) | copy-start | bytes 3076
  14.6 69.9 %all-to-all-start = ((bf16[16,36,2048]{2,1,0:T(8,128)(2,1)}), bf16[16,36,2048]{2,1,0:T(8,128)(2,1)S(1)}, u32[]{:S(2)}, u32[]{:S(2)}) async-start(bf16[16,36,2048]{2,1,0:T(8,128)(2,1)} %bitcast.161), calls=%async_computation | async-start | bytes 5242880 | tf_op jit(solution)/shard_map/all_to_all | solution.py:140
  87.6 65.3 %all-to-all-start.4 = ((bf16[16,36,2048]{2,1,0:T(8,128)(2,1)}), bf16[16,36,2048]{2,1,0:T(8,128)(2,1)}, u32[]{:S(2)}, u32[]{:S(2)}) async-start(bf16[16,36,2048]{2,1,0:T(8,128)(2,1)} %bitcast.160), calls=%async_computation.4 | async-start | bytes 5242880 | tf_op jit(solution)/shard_map/all_to_all | solution.py:267
  93.0 89.0 %all-gather.3.cloned.1.call-start = ((), (), s32[]{:S(2)}) async-start(), calls=%async_computation.13 | async-start | bytes 3932160 | tf_op jit(solution)/shard_map/all_gather | solution.py:125
  154.2 24.1 %all-to-all-start.1 = ((bf16[4,1,1,384,512]{3,4,2,1,0:T(8,128)(2,1)}), bf16[4,1,1,384,512]{3,4,2,1,0:T(8,128)(2,1)}, u32[]{:S(2)}, u32[]{:S(2)}) async-start(bf16[4,1,1,384,512]{3,4,2,1,0:T(8,128)(2,1)} %stack.10), calls=%async_computation.1 | async-start | bytes 3145728 | tf_op jit(solution)/shard_map/all_to_all | solution.py:17
  158.5 127.3 %reduce-scatter.2.cloned.1.call-start = ((), (), s32[]{:S(2)}) async-start(), calls=%async_computation.14 | async-start | bytes 5898240 | tf_op jit(solution)/shard_map/reduce_scatter | solution.py:54
  189.0 8.9 %copy-start.21 = (bf16[576,384]{1,0:T(8,128)(2,1)}, bf16[576,384]{1,0:T(8,128)(2,1)S(1)}, u32[]{:S(2)}) copy-start(bf16[576,384]{1,0:T(8,128)(2,1)S(1)} %get-tuple-element.37) | copy-start | bytes 1327108
  294.7 4.7 copy-start.13
  307.5 38.2 %all-to-all-start.5 = ((bf16[16,2,18432]{2,1,0:T(2,128)(2,1)}), bf16[16,2,18432]{2,1,0:T(2,128)(2,1)S(1)}, u32[]{:S(2)}, u32[]{:S(2)}) async-start(bf16[16,2,18432]{2,1,0:T(2,128)(2,1)} %reshape.678), calls=%async_computation.6 | async-start | bytes 2359296 | tf_op jit(solution)/shard_map/all_to_all | solution.py:28
  323.7 27.9 %copy-start.29 = (s32[1,8]{1,0:T(1,128)S(1)}, s32[1,8]{1,0:T(1,128)}, u32[]{:S(2)}) copy-start(s32[1,8]{1,0:T(1,128)} %param.25) | copy-start | bytes 100
  346.7 63.9 %all-to-all-start.2 = ((bf16[16,36,2048]{2,1,0:T(8,128)(2,1)}), bf16[16,36,2048]{2,1,0:T(8,128)(2,1)}, u32[]{:S(2)}, u32[]{:S(2)}) async-start(bf16[16,36,2048]{2,1,0:T(8,128)(2,1)} %reshape.552), calls=%async_computation.2 | async-start | bytes 5242880 | tf_op jit(solution)/shard_map/all_to_all | solution.py:153
  410.7 20.0 %all-to-all-start.7 = ((bf16[16,2,6144]{2,1,0:T(2,128)(2,1)}), bf16[16,2,6144]{2,1,0:T(2,128)(2,1)S(1)}, u32[]{:S(2)}, u32[]{:S(2)}) async-start(bf16[16,2,6144]{2,1,0:T(2,128)(2,1)} %reshape.680), calls=%async_computation.8 | async-start | bytes 786432 | tf_op jit(solution)/shard_map/all_to_all | solution.py:195
  416.4 19.3 %copy-start.15 = (bf16[16,12288]{1,0:T(8,128)(2,1)S(1)}, bf16[16,12288]{1,0:T(8,128)(2,1)}, u32[]{:S(2)}) copy-start(bf16[16,12288]{1,0:T(8,128)(2,1)} %reshape.576) | copy-start | bytes 1179652
  431.4 25.9 %all-to-all-start.6 = ((bf16[16,2,12288]{2,1,0:T(2,128)(2,1)}), bf16[16,2,12288]{2,1,0:T(2,128)(2,1)}, u32[]{:S(2)}, u32[]{:S(2)}) async-start(bf16[16,2,12288]{2,1,0:T(2,128)(2,1)} %reshape.682), calls=%async_computation.7 | async-start | bytes 1572864 | tf_op jit(solution)/shard_map/all_to_all | solution.py:192
  444.5 17.5 %copy-start.27 = (s32[1,128,2]{1,2,0:T(2,128)S(1)}, s32[1,128,2]{1,2,0:T(2,128)}, u32[]{:S(2)}) copy-start(s32[1,128,2]{1,2,0:T(2,128)} %param.23) | copy-start | bytes 3076
  457.4 57.7 %all-to-all-start.10 = ((bf16[16,2,36864]{2,1,0:T(2,128)(2,1)}), bf16[16,2,36864]{2,1,0:T(2,128)(2,1)}, u32[]{:S(2)}, u32[]{:S(2)}) async-start(bf16[16,2,36864]{2,1,0:T(2,128)(2,1)} %reshape.684), calls=%async_computation.11 | async-start | bytes 4718592 | tf_op jit(solution)/shard_map/all_to_all | solution.py:28
  461.7 167.0 %all-gather.5.cloned.1.call-start = ((), (), s32[]{:S(2)}) async-start(), calls=%async_computation.15 | async-start | bytes 3932160 | tf_op jit(solution)/shard_map/all_gather | solution.py:125
  474.8 4.6 slice-start
  474.8 18.4 %copy-start.24 = (f32[1,2048]{1,0:T(1,128)S(1)}, f32[1,2048]{1,0:T(1,128)}, u32[]{:S(2)}) copy-start(f32[1,2048]{1,0:T(1,128)} %param.20) | copy-start | bytes 24580
  478.1 14.9 %collective-permute-start = (bf16[128,2048]{1,0:T(8,128)(2,1)S(1)}, bf16[128,2048]{1,0:T(8,128)(2,1)S(1)}, u32[]{:S(2)}, u32[]{:S(2)}) collective-permute-start(bf16[128,2048]{1,0:T(8,128)(2,1)S(1)} %fusion.34), channel_id=1, source_target_pairs={{192,0},{0,64},{64,128},{128,192},{193,1},{1,65},{65,129},{129,193... | collective-permute-start | bytes 1572872 | tf_op jit(solution)/shard_map/ppermute | solution.py:65
  479.8 15.4 %copy-start.18 = (bf16[16,2,6144]{2,1,0:T(2,128)(2,1)S(1)}, bf16[16,2,6144]{2,1,0:T(2,128)(2,1)}, u32[]{:S(2)}) copy-start(bf16[16,2,6144]{2,1,0:T(2,128)(2,1)} %copy-done.17) | copy-start | bytes 1179652
  495.6 7.8 %copy-start.4 = (bf16[16,1,12288]{2,1,0:T(2,128)(2,1)}, bf16[16,1,12288]{2,1,0:T(2,128)(2,1)S(1)}, u32[]{:S(2)}) copy-start(bf16[16,1,12288]{2,1,0:T(2,128)(2,1)S(1)} %reshape.681) | copy-start | bytes 1179652
  509.1 6.0 copy-start.6
  516.9 65.6 %all-to-all-start.3 = ((bf16[16,36,2048]{2,1,0:T(8,128)(2,1)}), bf16[16,36,2048]{2,1,0:T(8,128)(2,1)}, u32[]{:S(2)}, u32[]{:S(2)}) async-start(bf16[16,36,2048]{2,1,0:T(8,128)(2,1)} %bitcast.18), calls=%async_computation.3 | async-start | bytes 5242880 | tf_op jit(solution)/shard_map/all_to_all | solution.py:140
  542.3 40.2 %copy-start.19 = (bf16[384,512]{0,1:T(8,128)(2,1)S(1)}, bf16[384,512]{0,1:T(8,128)(2,1)}, u32[]{:S(2)}) copy-start(bf16[384,512]{0,1:T(8,128)(2,1)} %copy.93) | copy-start | bytes 1179652
  544.5 43.6 %copy-start.16 = (bf16[16,12288]{1,0:T(8,128)(2,1)S(1)}, bf16[16,12288]{1,0:T(8,128)(2,1)}, u32[]{:S(2)}) copy-start(bf16[16,12288]{1,0:T(8,128)(2,1)} %get-tuple-element.36) | copy-start | bytes 1179652
  583.7 24.3 %all-to-all-start.8 = ((bf16[4,1,1,384,512]{3,4,2,1,0:T(8,128)(2,1)}), bf16[4,1,1,384,512]{3,4,2,1,0:T(8,128)(2,1)}, u32[]{:S(2)}, u32[]{:S(2)}) async-start(bf16[4,1,1,384,512]{3,4,2,1,0:T(8,128)(2,1)} %stack.27), calls=%async_computation.9 | async-start | bytes 3145728 | tf_op jit(solution)/shard_map/all_to_all | solution.py:17
  597.0 18.2 %copy-start.28 = (f32[1,128,2]{1,2,0:T(2,128)S(1)}, f32[1,128,2]{1,2,0:T(2,128)}, u32[]{:S(2)}) copy-start(f32[1,128,2]{1,2,0:T(2,128)} %param.24) | copy-start | bytes 3076
  608.1 61.1 %all-to-all-start.11 = ((bf16[16,2,36864]{2,1,0:T(2,128)(2,1)}), bf16[16,2,36864]{2,1,0:T(2,128)(2,1)S(1)}, u32[]{:S(2)}, u32[]{:S(2)}) async-start(bf16[16,2,36864]{2,1,0:T(2,128)(2,1)} %reshape.686), calls=%async_computation.12 | async-start | bytes 4718592 | tf_op jit(solution)/shard_map/all_to_all | solution.py:28
  670.6 65.2 %all-to-all-start.9 = ((bf16[16,36,2048]{2,1,0:T(8,128)(2,1)}), bf16[16,36,2048]{2,1,0:T(8,128)(2,1)S(1)}, u32[]{:S(2)}, u32[]{:S(2)}) async-start(bf16[16,36,2048]{2,1,0:T(8,128)(2,1)} %reshape.569), calls=%async_computation.10 | async-start | bytes 5242880 | tf_op jit(solution)/shard_map/all_to_all | solution.py:153
  742.5 6.7 copy-start.1
  (17 other events, 42.8 us)
Sparse Core Ops, SparseCore 0:
  96.2 43.1 all-gather.2
  233.4 52.4 reduce-scatter.1
  511.7 39.5 all-gather.4
